TPU v7x, 128 devices: a whole 4x4x4 slice. The times are simulated.
128 devices in a mesh: fsdp: 4 (over z_hi, core), ctx: 32 (over z_lo, x, y).
Axes of the slice: x: 4, y: 4, z: 4 (z_hi: 2, z_lo: 2; z = z_hi * 2 + z_lo), core: 2. Of those that a mesh axis runs over, the one named last changes fastest.
Arguments:
- tokens: bfloat16 [4, 16384, 8192], P('fsdp', 'ctx'), may hold values from -56 to 56
- codes: int32 [128, 20480], P('fsdp'), may hold values from 0 to 65535
- scales: bfloat16 [128, 1280], P('fsdp'), may hold values from 0.0039978027 to 0.039794922
- down_adapter_matrix: bfloat16 [128, 4096], P('fsdp'), may hold values from -0.0625 to 0.0625
- up_adapter_matrix: bfloat16 [64, 1280], replicated, may hold values from -0.75 to 0.75
- positions: int32 [4, 16384], P('fsdp', 'ctx'), may hold values from 0 to 16383, as said below
Outputs:
- attended: bfloat16 [4, 16384, 1024], P('fsdp', 'ctx')
Inputs may be any that keep to these rules, and one draw needn't show every extreme that they name: In each sequence the first and the last 256 tokens of each device's share hold consecutive increasing positions, of some block a and of block 63 - a of the sequence (blocks of 256 positions), a different a on each device of a sequence; every position of 0 to 16383 appears once in each sequence.
All inputs are finite; a program needn't handle non-finite values.
Results may differ from a plain program's by a relative error of at most 0.014.
Values may be sent and summed in bfloat16 or wider, within the bound.
A program may use at most 192 MiB of HBM per device.

v0:
```python
import jax
import jax.numpy as jnp
from jax import lax
from jax.sharding import PartitionSpec as P

QH = 8
HD = 128
normal_float_levels = [
    -1.0,
    -0.6961928009986877,
    -0.5250730514526367,
    -0.39491748809814453,
    -0.28444138169288635,
    -0.18477343022823334,
    -0.09105003625154495,
    0.0,
    0.07958029955625534,
    0.16093020141124725,
    0.24611230194568634,
    0.33791524171829224,
    0.44070982933044434,
    0.5626170039176941,
    0.7229568362236023,
    1.0,
]
rope_base = 500000.0
adapter_scaling = 0.5


def unpack_codes(packed):
    blocks = packed.shape[0]
    words = packed.reshape(blocks, 64, -1)
    nibbles = [jnp.remainder(jnp.floor_divide(words, 16**place), 16) for place in range(4)]
    return jnp.stack(nibbles, axis=-1).reshape(blocks, 64, -1)


def pick_level(code_full):
    bit_flags = [jnp.remainder(jnp.floor_divide(code_full, 2**place), 2) == 1 for place in range(4)]
    current = [jnp.float32(level) for level in normal_float_levels]
    for place in range(4):
        current = [
            jnp.where(bit_flags[place], current[2 * pair + 1], current[2 * pair])
            for pair in range(len(current) // 2)
        ]
    return current[0]


def dequantize(packed, block_scales):
    code_full = unpack_codes(packed)
    values = pick_level(code_full)
    scaled = values * block_scales.astype(jnp.float32)[:, None, :]
    return scaled.reshape(-1, scaled.shape[-1]).astype(jnp.bfloat16)


def rotate_pairs(values, angles):
    half_size = values.shape[-1] // 2
    first_half = values[..., :half_size]
    second_half = values[..., half_size:]
    cosine = jnp.cos(angles)
    sine = jnp.sin(angles)
    return jnp.concatenate(
        [first_half * cosine - second_half * sine, second_half * cosine + first_half * sine],
        axis=-1,
    )


def make_angles(token_position):
    half_size = HD // 2
    steps_idx = jnp.arange(half_size, dtype=jnp.float32)
    inverse = jnp.exp(-jnp.log(jnp.float32(rope_base)) * 2.0 * steps_idx / HD)
    return token_position.astype(jnp.float32)[:, None] * inverse[None, :]


def tile_update(state, query_part, query_pos, tile, tile_pos):
    running_max, running_sum, running_acc = state
    scores = jnp.einsum("hqd,kd->hqk", query_part, tile[:, :HD], preferred_element_type=jnp.float32)
    scores = jnp.where(tile_pos[None, None, :] <= query_pos[None, :, None], scores, -jnp.inf)
    new_max = jnp.maximum(running_max, jnp.max(scores, axis=-1))
    factor = jnp.exp(running_max - new_max)
    expo = jnp.exp(scores - new_max[..., None])
    new_sum = running_sum * factor + jnp.sum(expo, axis=-1)
    weights = expo.astype(jnp.bfloat16)
    new_acc = running_acc * factor[..., None] + jnp.einsum(
        "hqk,kd->hqd", weights, tile[:, HD:], preferred_element_type=jnp.float32
    )
    return (new_max, new_sum, new_acc)


def on_device(tokens, codes, scales, down_adapter_matrix, up_adapter_matrix, positions):
    local_tokens = tokens[0]
    local_pos = positions[0]
    tok_count = local_tokens.shape[0]
    adapter_rank_size = up_adapter_matrix.shape[0]
    input_width = up_adapter_matrix.shape[1]
    own_weight = dequantize(codes, scales).reshape(scales.shape[0], 64 * input_width)
    weight_piece = lax.all_gather(own_weight, "fsdp", axis=0, tiled=True)
    adapter_slice = lax.all_gather(down_adapter_matrix, "fsdp", axis=0, tiled=True)
    rows = weight_piece.shape[0] * 64
    first_total = jnp.dot(
        local_tokens, weight_piece.reshape(rows, input_width), preferred_element_type=jnp.float32
    )
    second_total = jnp.dot(
        local_tokens,
        adapter_slice.reshape(rows, adapter_rank_size),
        preferred_element_type=jnp.float32,
    )
    low_rank_output = second_total.astype(jnp.bfloat16)
    joined_output = first_total + adapter_scaling * jnp.dot(
        low_rank_output, up_adapter_matrix, preferred_element_type=jnp.float32
    )
    angles = make_angles(local_pos)
    qwidth = QH * HD
    query_output = joined_output[:, :qwidth].reshape(tok_count, QH, HD).transpose(1, 0, 2)
    query_output = (rotate_pairs(query_output, angles) * HD ** (-0.5)).astype(jnp.bfloat16)
    key = rotate_pairs(joined_output[:, qwidth : qwidth + HD], angles).astype(jnp.bfloat16)
    value_output = joined_output[:, qwidth + HD :].astype(jnp.bfloat16)
    keys_values = jnp.concatenate([key, value_output], axis=1)
    all_positions = lax.all_gather(local_pos, "ctx", axis=0, tiled=True)
    half_size = tok_count // 2
    query_parts = (query_output[:, :half_size], query_output[:, half_size:])
    pos_parts = (local_pos[:half_size], local_pos[half_size:])
    empty_state = (
        jnp.full((QH, half_size), -1e30, jnp.float32),
        jnp.zeros((QH, half_size), jnp.float32),
        jnp.zeros((QH, half_size, HD), jnp.float32),
    )
    states = (empty_state, empty_state)
    piece = lax.all_gather(keys_values, "ctx", axis=0, tiled=True)
    count = piece.shape[0]

    def one_tile(carry, tile_idx):
        tile = lax.dynamic_slice_in_dim(piece, tile_idx * half_size, half_size, 0)
        tile_pos = lax.dynamic_slice_in_dim(all_positions, tile_idx * half_size, half_size, 0)
        updated = []
        for part_idx in range(2):

            def apply_tile(state, part_idx=part_idx):
                return tile_update(
                    state, query_parts[part_idx], pos_parts[part_idx], tile, tile_pos
                )

            def keep_state(state):
                return state

            visible = jnp.min(tile_pos) <= jnp.max(pos_parts[part_idx])
            updated.append(lax.cond(visible, apply_tile, keep_state, carry[part_idx]))
        return ((updated[0], updated[1]), None)

    states, unused = lax.scan(one_tile, states, jnp.arange(count // half_size, dtype=jnp.int32))
    halves = [states[part_idx][2] / states[part_idx][1][..., None] for part_idx in range(2)]
    combined = jnp.concatenate(halves, axis=1)
    attended = combined.transpose(1, 0, 2).reshape(tok_count, QH * HD).astype(jnp.bfloat16)
    return attended[None]


def solution(mesh):
    in_specs = (
        P("fsdp", "ctx", None),
        P("fsdp", None),
        P("fsdp", None),
        P("fsdp", None),
        P(),
        P("fsdp", "ctx"),
    )
    out_specs = P("fsdp", "ctx", None)
    return jax.shard_map(
        on_device, mesh=mesh, in_specs=in_specs, out_specs=out_specs, check_vma=False
    )
```

profile of v0, /device:TPU:0, one launch (start us, length us, event | category | flops | bytes accessed | tf_op | source)
XLA Modules:
  0.0 1176.6 jit_solution(5774909089922595813)
XLA Ops:
  7.3 2.8 reshape.460
  10.1 8.5 add_select_fusion.13
  18.6 5.6 pad_add_fusion
  24.2 28.0 %copy.44 = s32[32,64,320,4]{0,3,2,1:T(4,128)} copy(s32[32,64,320,4]{2,1,3,0:T(8,128)} %pad_add_fusion) | data formatting | bytes 20971520 | tf_op jit(solution)/shard_map/stack | solution.py:34
  52.4 151.2 %fusion.33 = bf16[32,81920]{0,1:T(8,128)(2,1)} fusion(s32[32,81920]{0,1:T(8,128)} %bitcast.50, f32[32,1280]{0,1:T(8,128)S(1)} %copy.45), kind=kLoop, calls=%fused_computation.65 | loop fusion | flops 243793920 | bytes 15892480 | tf_op jit(solution)/shard_map/convert_element_type | solution.py:52
  203.6 17.3 %copy.46 = bf16[32,81920]{1,0:T(8,128)(2,1)} copy(bf16[32,81920]{0,1:T(8,128)(2,1)} %fusion.33) | data formatting | bytes 10485760 | tf_op jit(solution)/shard_map/convert_element_type | solution.py:52
  221.7 4.3 reshape.463
  225.9 133.4 %all-gather.5.cloned.1.call-done = bf16[128,81920]{1,0:T(8,128)(2,1)} async-done(((bf16[32,81920]{1,0:T(8,128)(2,1)}), bf16[128,81920]{1,0:T(8,128)(2,1)}) %all-gather.5.cloned.1.call-update) | async-done | bytes 20971536 | tf_op jit(solution)/shard_map/all_gather | solution.py:96
  359.4 23.6 %reshape.462 = bf16[8192,1280]{1,0:T(8,128)(2,1)} reshape(bf16[128,81920]{1,0:T(8,128)(2,1)} %all-gather.5.cloned.1.call-done) | data formatting | bytes 41943040 | tf_op jit(solution)/shard_map/reshape | solution.py:100
  383.0 18.7 %fusion.41 = f32[512,1280]{0,1:T(8,128)} fusion(bf16[8192,1280]{1,0:T(8,128)(2,1)} %reshape.462, bf16[1,512,8192]{2,1,0:T(8,128)(2,1)} %param.12), kind=kOutput, calls=%fused_computation.96 | convolution fusion | flops 10737418240 | bytes 31981568 | tf_op jit(solution)/shard_map/dot_general | solution.py:99
  401.7 7.9 fusion.40
  411.0 80.8 %all-gather = s32[1,16384]{1,0:T(1,128)S(1)} all-gather(s32[1,512]{1,0:T(1,128)S(1)} %copy-done.2), channel_id=2, replica_groups=mesh['fsdp'=4,'ctx'=32] {'ctx'}, dimensions={1}, use_global_device_ids=true | all-gather | bytes 67584 | tf_op jit(solution)/shard_map/all_gather | solution.py:118
  497.8 78.2 %all-gather.9.cloned.1.call-done = bf16[16384,256]{0,1:T(8,128)(2,1)} async-done(((bf16[512,256]{0,1:T(8,128)(2,1)}), bf16[16384,256]{0,1:T(8,128)(2,1)}) %all-gather.9.cloned.1.call-update) | async-done | bytes 8388624 | tf_op jit(solution)/shard_map/all_gather | solution.py:128
  576.2 591.1 %while.21 = (s32[]{:T(128)}, f32[8,256]{1,0:T(8,128)S(1)}, f32[8,256]{1,0:T(8,128)S(1)}, f32[8,256,128]{2,1,0:T(8,128)S(1)}, f32[8,256]{1,0:T(8,128)S(1)}, /*ind...) while((s32[]{:T(128)}, f32[8,256]{1,0:T(8,128)S(1)}, ...), condition=%wide.region_12.13_spmd, body=%wide.region_2.0_spmd.sunk | while | flops 546447616 | bytes 19405304 | solution.py:149
  582.1 2.0 conditional.5
  611.7 2.0 conditional.5
  620.9 2.0 conditional.5
  630.1 2.0 conditional.5
  639.3 2.0 conditional.5
  648.5 2.0 conditional.5
  657.7 2.0 conditional.5
  666.9 2.0 conditional.5
  676.1 2.0 conditional.5
  685.3 2.0 conditional.5
  703.8 2.0 conditional.5
  722.2 2.0 conditional.5
  731.4 2.0 conditional.5
  759.0 2.0 conditional.5
  768.2 2.0 conditional.5
  777.4 2.0 conditional.5
  786.6 2.0 conditional.5
  823.4 2.0 conditional.5
  841.8 2.0 conditional.5
  860.2 2.0 conditional.5
  878.6 2.0 conditional.5
  906.2 2.0 conditional.5
  915.5 2.0 conditional.5
  924.7 2.0 conditional.5
  933.9 2.0 conditional.5
  943.1 2.0 conditional.5
  952.3 2.0 conditional.5
  961.5 2.0 conditional.5
  1035.1 2.0 conditional.5
  1053.5 2.0 conditional.5
  1071.9 2.0 conditional.5
  1117.9 2.0 conditional.5
  1136.4 2.0 conditional.5
  1154.8 2.0 conditional.5
  (843 shorter events, 452.7 us)
Async XLA Ops:
  6.5 395.2 %copy-start = (bf16[64,1280]{1,0:T(8,128)(2,1)S(1)}, bf16[64,1280]{1,0:T(8,128)(2,1)}, u32[]{:S(2)}) copy-start(bf16[64,1280]{1,0:T(8,128)(2,1)} %param.16) | copy-start | bytes 491524
  6.5 215.1 %all-gather.7.cloned.1.call-start = ((), (), s32[]{:S(2)}) async-start(), calls=%async_computation.1 | async-start | bytes 1310720 | tf_op jit(solution)/shard_map/all_gather | solution.py:97
  7.3 352.1 %all-gather.5.cloned.1.call-start = ((), (), s32[]{:S(2)}) async-start(), calls=%async_computation | async-start | bytes 26214400 | tf_op jit(solution)/shard_map/all_gather | solution.py:96
  24.2 28.0 %copy-start.1 = (bf16[32,1280]{1,0:T(8,128)(2,1)S(1)}, bf16[32,1280]{1,0:T(8,128)(2,1)}, u32[]{:S(2)}) copy-start(bf16[32,1280]{1,0:T(8,128)(2,1)} %param.14) | copy-start | bytes 245764
  220.9 0.7 copy-start.2
  221.0 355.1 %all-gather.9.cloned.1.call-start = ((), (), s32[]{:S(2)}) async-start(), calls=%async_computation.2 | async-start | bytes 8650752 | tf_op jit(solution)/shard_map/all_gather | solution.py:128
Sparse Core Ops, SparseCore 0:
  9.0 23.3 all-gather.6
  221.1 138.2 all-gather.4
  411.1 164.9 all-gather.8
where the time goes:
time: 1180 us
  local copies, waits for them, and re-layouts  285 us (24%)
  other arithmetic  251 us (21%)
  loops' own time  213 us (18%)
  waiting for transfers between devices  212 us (18%)
  matrix products  121 us (10%)
  blocking collectives  80.8 us (7%)
  between operations  13.3 us (1%)
    another operation x1, loops' own time, on_device(): lax.scan(one_tile, states, jnp.arange(count // half_size, dtype=jnp.int32))  208 us
    dynamic_slice x128, local copies, waits for them, and re-layouts, one_tile(): tile = lax.dynamic_slice_in_dim(piece, tile_idx * half_size, half_size, 0)  164 us
    convert_element_type x1, other arithmetic, dequantize(): return scaled.reshape(-1, scaled.shape[-1]).astype(jnp.bfloat16)  151 us
    all_gather x1, waiting for transfers between devices, on_device(): weight_piece = lax.all_gather(own_weight, 'fsdp', axis=0, tiled=True)  133 us
    all_gather x1, blocking collectives, on_device(): all_positions = lax.all_gather(local_pos, 'ctx', axis=0, tiled=True)  80.8 us
    all_gather x1, waiting for transfers between devices, on_device(): piece = lax.all_gather(keys_values, 'ctx', axis=0, tiled=True)  78.2 us
    dot_general x65, matrix products, tile_update(): jnp.einsum('hqk,kd->hqd', weights, tile[:, HD:], preferred_element_type=j...  65.4 us
    reduce_min x64, other arithmetic, one_tile(): visible = jnp.min(tile_pos) <= jnp.max(pos_parts[part_idx])  49.6 us
  transfers between devices with their start and end apart: 3, of which 2 were waited for; matrix products, arithmetic and copies ran while one was open for 19% of the time, Pallas kernels for 0%

commit v1 on v0

--- a/solution.py
+++ b/solution.py
@@ -125,7 +125,9 @@
         jnp.zeros((QH, half_size, HD), jnp.float32),
     )
     states = (empty_state, empty_state)
-    piece = lax.all_gather(keys_values, "ctx", axis=0, tiled=True)
+    piece = jnp.concatenate(
+        lax.all_to_all(jnp.stack([keys_values] * lax.axis_size("ctx")), "ctx", 0, 0), axis=0
+    )
     count = piece.shape[0]
 
     def one_tile(carry, tile_idx):

time: 1180 us -> 1130 us (0.958)
  blocking collectives: 80.8 us -> 191 us
  local copies, waits for them, and re-layouts: 285 us -> 188 us
  waiting for transfers between devices: 212 us -> 135 us
    all_gather x1, blocking collectives: 80.8 us -> 191 us  [on_device(): all_positions = lax.all_gather(local_pos, 'ctx', axis=0, tiled=True)]
    dynamic_slice x128 -> x64, local copies, waits for them, and re-layouts: 164 us -> 58.4 us  [one_tile(): tile = lax.dynamic_slice_in_dim(piece, tile_idx * half_size, half_size, 0)]
    all_gather x1 -> x0, waiting for transfers between devices: 78.2 us -> none  [on_device(): piece = lax.all_gather(keys_values, 'ctx', axis=0, tiled=True)]
  transfers between devices with their start and end apart: 3 -> 3, of which waited for: 2 -> 1; matrix products, arithmetic and copies ran while one was open for 19% -> 20% of each run, Pallas kernels for 0% -> 0%
where the time goes in v1:
time: 1130 us; the launch traced here: 1120 us
  other arithmetic  251 us (22%)
  loops' own time  212 us (19%)
  blocking collectives  191 us (17%)
  local copies, waits for them, and re-layouts  188 us (17%)
  waiting for transfers between devices  135 us (12%)
  matrix products  122 us (11%)
  between operations  13.6 us (1%)
    another operation x1, loops' own time, on_device(): lax.scan(one_tile, states, jnp.arange(count // half_size, dtype=jnp.int32))  207 us
    all_gather x1, blocking collectives, on_device(): all_positions = lax.all_gather(local_pos, 'ctx', axis=0, tiled=True)  191 us
    convert_element_type x1, other arithmetic, dequantize(): return scaled.reshape(-1, scaled.shape[-1]).astype(jnp.bfloat16)  151 us
    all_gather x1, waiting for transfers between devices, on_device(): weight_piece = lax.all_gather(own_weight, 'fsdp', axis=0, tiled=True)  134 us
    dot_general x65, matrix products, tile_update(): jnp.einsum('hqk,kd->hqd', weights, tile[:, HD:], preferred_element_type=j...  65.4 us
    dynamic_slice x64, local copies, waits for them, and re-layouts, one_tile(): tile = lax.dynamic_slice_in_dim(piece, tile_idx * half_size, half_size, 0)  58.4 us
    reduce_min x64, other arithmetic, one_tile(): visible = jnp.min(tile_pos) <= jnp.max(pos_parts[part_idx])  47.4 us
    dynamic_slice x64, local copies, waits for them, and re-layouts, on_device(): lax.scan(one_tile, states, jnp.arange(count // half_size, dtype=jnp.int32))  39.7 us
  transfers between devices with their start and end apart: 3, of which 1 were waited for; matrix products, arithmetic and copies ran while one was open for 20% of the time, Pallas kernels for 0%

profile of v1, /device:TPU:0, one launch (start us, length us, event | category | flops | bytes accessed | tf_op | source)
XLA Modules:
  0.0 1119.6 jit_solution(454780429832980708)
XLA Ops:
  7.3 4.0 reshape.465
  11.3 9.6 add_select_fusion.13
  20.9 5.6 pad_add_fusion
  26.5 28.0 %copy.44 = s32[32,64,320,4]{0,3,2,1:T(4,128)} copy(s32[32,64,320,4]{2,1,3,0:T(8,128)} %pad_add_fusion) | data formatting | bytes 20971520 | tf_op jit(solution)/shard_map/stack | solution.py:34
  54.6 151.3 %fusion.33 = bf16[32,81920]{0,1:T(8,128)(2,1)} fusion(s32[32,81920]{0,1:T(8,128)} %bitcast.51, f32[32,1280]{0,1:T(8,128)S(1)} %copy.45), kind=kLoop, calls=%fused_computation.65 | loop fusion | flops 243793920 | bytes 15892480 | tf_op jit(solution)/shard_map/convert_element_type | solution.py:52
  205.9 17.3 %copy.46 = bf16[32,81920]{1,0:T(8,128)(2,1)} copy(bf16[32,81920]{0,1:T(8,128)(2,1)} %fusion.33) | data formatting | bytes 10485760 | tf_op jit(solution)/shard_map/convert_element_type | solution.py:52
  224.0 3.3 reshape.468
  227.2 134.4 %all-gather.4.cloned.1.call-done = bf16[128,81920]{1,0:T(8,128)(2,1)} async-done(((bf16[32,81920]{1,0:T(8,128)(2,1)}), bf16[128,81920]{1,0:T(8,128)(2,1)}) %all-gather.4.cloned.1.call-update) | async-done | bytes 20971536 | tf_op jit(solution)/shard_map/all_gather | solution.py:96
  361.7 23.6 %reshape.467 = bf16[8192,1280]{1,0:T(8,128)(2,1)} reshape(bf16[128,81920]{1,0:T(8,128)(2,1)} %all-gather.4.cloned.1.call-done) | data formatting | bytes 41943040 | tf_op jit(solution)/shard_map/reshape | solution.py:100
  385.3 18.7 %fusion.41 = f32[512,1280]{0,1:T(8,128)} fusion(bf16[8192,1280]{1,0:T(8,128)(2,1)} %reshape.467, bf16[1,512,8192]{2,1,0:T(8,128)(2,1)} %param.12), kind=kOutput, calls=%fused_computation.96 | convolution fusion | flops 10737418240 | bytes 31981568 | tf_op jit(solution)/shard_map/dot_general | solution.py:99
  404.0 8.8 fusion.40
  415.4 4.2 stack.5
  419.6 7.3 all-to-all-start
  426.9 190.6 %all-gather = s32[1,16384]{1,0:T(1,128)S(1)} all-gather(s32[1,512]{1,0:T(1,128)S(1)} %copy-done.2), channel_id=2, replica_groups=mesh['fsdp'=4,'ctx'=32] {'ctx'}, dimensions={1}, use_global_device_ids=true | all-gather | bytes 67584 | tf_op jit(solution)/shard_map/all_gather | solution.py:118
  618.2 3.1 slice.67
  621.6 2.1 copy.49
  625.6 484.4 %while.21 = (s32[]{:T(128)}, f32[8,256]{1,0:T(8,128)S(1)}, f32[8,256]{1,0:T(8,128)S(1)}, f32[8,256,128]{2,1,0:T(8,128)S(1)}, f32[8,256]{1,0:T(8,128)S(1)}, /*ind...) while((s32[]{:T(128)}, f32[8,256]{1,0:T(8,128)S(1)}, ...), condition=%wide.region_12.13_spmd, body=%wide.region_2.0_spmd.sunk | while | flops 546447616 | bytes 19143160 | solution.py:151
  629.8 2.0 conditional.5
  639.4 2.0 conditional.5
  646.9 2.0 conditional.5
  654.5 2.0 conditional.5
  662.0 2.0 conditional.5
  669.5 2.0 conditional.5
  677.1 2.0 conditional.5
  684.6 2.0 conditional.5
  692.1 2.0 conditional.5
  699.7 2.0 conditional.5
  707.2 2.0 conditional.5
  714.7 2.0 conditional.5
  722.3 2.0 conditional.5
  729.8 2.0 conditional.5
  737.4 2.0 conditional.5
  744.9 2.0 conditional.5
  752.4 2.0 conditional.5
  775.0 2.0 conditional.5
  782.6 2.0 conditional.5
  790.1 2.0 conditional.5
  797.7 2.0 conditional.5
  820.3 2.0 conditional.5
  827.8 2.0 conditional.5
  835.3 2.0 conditional.5
  842.9 2.0 conditional.5
  850.4 2.0 conditional.5
  857.9 2.0 conditional.5
  895.6 2.0 conditional.5
  903.2 2.0 conditional.5
  971.0 2.0 conditional.5
  1038.8 2.0 conditional.5
  (780 shorter events, 351.1 us)
Async XLA Ops:
  6.5 397.4 %copy-start = (bf16[64,1280]{1,0:T(8,128)(2,1)S(1)}, bf16[64,1280]{1,0:T(8,128)(2,1)}, u32[]{:S(2)}) copy-start(bf16[64,1280]{1,0:T(8,128)(2,1)} %param.16) | copy-start | bytes 491524
  6.5 217.4 %all-gather.6.cloned.1.call-start = ((), (), s32[]{:S(2)}) async-start(), calls=%async_computation.2 | async-start | bytes 1310720 | tf_op jit(solution)/shard_map/all_gather | solution.py:97
  7.3 354.4 %all-gather.4.cloned.1.call-start = ((), (), s32[]{:S(2)}) async-start(), calls=%async_computation.1 | async-start | bytes 26214400 | tf_op jit(solution)/shard_map/all_gather | solution.py:96
  26.5 28.0 %copy-start.1 = (bf16[32,1280]{1,0:T(8,128)(2,1)S(1)}, bf16[32,1280]{1,0:T(8,128)(2,1)}, u32[]{:S(2)}) copy-start(bf16[32,1280]{1,0:T(8,128)(2,1)} %param.14) | copy-start | bytes 245764
  223.2 0.7 copy-start.2
  419.6 205.8 %all-to-all-start = ((bf16[32,512,256]{2,1,0:T(8,128)(2,1)}), bf16[32,512,256]{2,1,0:T(8,128)(2,1)}, u32[]{:S(2)}, u32[]{:S(2)}) async-start(bf16[32,512,256]{2,1,0:T(8,128)(2,1)} %stack.5), calls=%async_computation | async-start | bytes 16777216 | tf_op jit(solution)/shard_map/all_to_all | solution.py:129
Sparse Core Ops, SparseCore 0:
  9.0 23.3 all-gather.5
  223.4 138.2 all-gather.3
